TPU v7x, 32 devices: a whole 2x2x4 slice. The times are simulated.
32 devices in a mesh: dp: 16 (over z, y, core), mp: 2 (over x).
Axes of the slice: x: 2, y: 2, z: 4, core: 2. Of those that a mesh axis runs over, the one named last changes fastest.
Arguments:
- tokens: bfloat16 [32768, 768], P('dp'), may hold values from -6 to 6
- grad_out: bfloat16 [32768, 768], P('dp'), may hold values from -6 to 6
- head_perm: int32 [32, 12], P('dp', 'mp'), may hold values from 0 to 1
- block_mask: int32 [32, 12, 3], P('dp', 'mp'), may hold values 0 or 1
- w_qkv: bfloat16 [768, 3, 768], P('dp', None, 'mp'), may hold values from -0.3125 to 0.3125
- b_qv: bfloat16 [2, 768], P(None, ('mp', 'dp')), may hold values from -3 to 3
- w_out: bfloat16 [768, 768], P('mp', 'dp'), may hold values from -0.625 to 0.625
- b_out: bfloat16 [768], P('dp'), may hold values from -3 to 3
- gain_one: bfloat16 [768], P('dp'), may hold values from 0.25 to 1.75
- shift_one: bfloat16 [768], P('dp'), may hold values from -2 to 2
- w_up: bfloat16 [768, 3072], P('dp', 'mp'), may hold values from -0.21875 to 0.21875
- b_up: bfloat16 [3072], P(('mp', 'dp')), may hold values from -3 to 3
- w_down: bfloat16 [3072, 768], P('mp', 'dp'), may hold values from -0.15625 to 0.15625
- b_down: bfloat16 [768], P('dp'), may hold values from -2 to 2
- gain_two: bfloat16 [768], P('dp'), may hold values from 0.25 to 1.75
- shift_two: bfloat16 [768], P('dp'), may hold values from -2 to 2
Outputs:
- output: bfloat16 [32768, 768], P('dp')
- input_grad: float32 [32768, 768], P('dp')
- grad_w_qkv: float32 [768, 3, 768], P('dp', None, 'mp')
- grad_b_qv: float32 [2, 768], P(None, ('mp', 'dp'))
- grad_w_out: float32 [768, 768], P('mp', 'dp')
- grad_b_out: float32 [768], P('dp')
- grad_gain_one: float32 [768], P('dp')
- grad_shift_one: float32 [768], P('dp')
- grad_w_up: float32 [768, 3072], P('dp', 'mp')
- grad_b_up: float32 [3072], P(('mp', 'dp'))
- grad_w_down: float32 [3072, 768], P('mp', 'dp')
- grad_b_down: float32 [768], P('dp')
- grad_gain_two: float32 [768], P('dp')
- grad_shift_two: float32 [768], P('dp')
Inputs may be any that keep to these rules, and one draw needn't show every extreme that they name: `head_perm`: 0 pairs each half with itself, 1 pairs it with the other half. `block_mask`: entry a + b is the keep flag of block a of the queries with block b of the keys (b <= a).
All inputs are finite; a program needn't handle non-finite values.
Results may differ from a plain program's by a relative error of at most 0.015.
The roundings to bfloat16 on the way count: a program that leaves them out, or rounds other values in their place, can miss the bound.
Values may be sent and summed in bfloat16 or wider, within the bound.
No kernel may reach another device: no remote copies, remote signals or barrier semaphores. Data moves between devices by JAX's collectives and lax.ppermute only.
A program may use at most 256 MiB of HBM per device.

v0:
```python
import jax
import jax.numpy as jnp
from jax import lax
from jax.sharding import PartitionSpec as P

HD = 64
norm_eps = 1e-05
masked_fill = -1e30


def layer_norm(hidden, gain_vec, shift_vec):
    centered = hidden - jnp.mean(hidden, axis=-1, keepdims=True)
    variance = jnp.mean(centered * centered, axis=-1, keepdims=True)
    return centered * lax.rsqrt(variance + norm_eps) * gain_vec + shift_vec


def gelu_exact(values):
    return jax.nn.gelu(values, approximate=False)


def contract_rows(first_mat, second_mat):
    return lax.dot_general(
        first_mat, second_mat, (((0,), (0,)), ((), ())), preferred_element_type=jnp.float32
    )


def contract_cols(first_mat, second_mat):
    return lax.dot_general(
        first_mat, second_mat, (((1,), (1,)), ((), ())), preferred_element_type=jnp.float32
    )


def pair_pattern(mask_rows, half_len, block_len):
    blocks = jnp.arange(half_len) // block_len
    row_block = blocks[:, None]
    col_block = blocks[None, :]
    entry_index = row_block + col_block
    chosen = jnp.zeros((mask_rows.shape[0], half_len, half_len), dtype=jnp.bool_)
    for entry_id in range(3):
        chosen = (
            chosen | (mask_rows[:, entry_id, None, None] == 1) & (entry_index == entry_id)[None]
        )
    allowed = chosen & (col_block <= row_block)[None]
    allowed_f = allowed.astype(jnp.float32)
    dead_f = 1.0 - jnp.max(allowed_f, axis=-1)
    return (allowed, allowed_f, dead_f)


def pair_keys(values, swapped):
    return jnp.where(swapped[None, :, None], jnp.roll(values, values.shape[0] // 2, axis=0), values)


def split_pairs(proj_low, perm_seq, head_count):
    seq_len = proj_low.shape[0]
    half_len = seq_len // 2
    split_heads = proj_low.reshape(seq_len, 3, head_count, HD)
    swapped = perm_seq == 1
    query_pair = split_heads[:, 0].reshape(2, half_len, head_count, HD)
    key_pair = pair_keys(split_heads[:, 1], swapped).reshape(2, half_len, head_count, HD)
    value_pair = pair_keys(split_heads[:, 2], swapped).reshape(2, half_len, head_count, HD)
    return (query_pair, key_pair, value_pair, swapped)


def masked_scores(query_pair, key_pair, allowed):
    raw_scores = jnp.einsum(
        "iqhd,ikhd->ihqk", query_pair, key_pair, preferred_element_type=jnp.float32
    ) * HD ** (-0.5)
    return jnp.where(allowed[None], raw_scores, masked_fill)


def forward_pass(tokens_seq, perm_seq, mask_seq, weights):
    (
        w_qkv,
        b_qv,
        w_out,
        b_out,
        gain_one,
        shift_one,
        w_up,
        b_up,
        w_down,
        b_down,
        gain_two,
        shift_two,
    ) = weights
    seq_len = tokens_seq.shape[0]
    half_len = seq_len // 2
    local_width = w_qkv.shape[2]
    head_count = local_width // HD
    projected = jnp.einsum("td,dcf->tcf", tokens_seq, w_qkv, preferred_element_type=jnp.float32)
    bias_rows = jnp.stack([b_qv[0], jnp.zeros_like(b_qv[0]), b_qv[1]]).astype(jnp.float32)
    proj_low = (projected + bias_rows[None]).astype(jnp.bfloat16)
    query_pair, key_pair, value_pair, swapped = split_pairs(proj_low, perm_seq, head_count)
    allowed, allowed_f, dead_f = pair_pattern(mask_seq, half_len, half_len // 2)
    masked = masked_scores(query_pair, key_pair, allowed)
    row_max = jnp.max(masked, axis=-1)
    row_total = jnp.sum(jnp.exp(masked - row_max[..., None]) * allowed_f[None], axis=-1)
    log_total = row_max + jnp.log(row_total + dead_f[None])
    attn_weights = (jnp.exp(masked - log_total[..., None]) * allowed_f[None]).astype(jnp.bfloat16)
    context = jnp.einsum(
        "ihqk,ikhd->iqhd", attn_weights, value_pair, preferred_element_type=jnp.float32
    )
    context_low = context.reshape(seq_len, local_width).astype(jnp.bfloat16)
    attn_part = jnp.dot(context_low, w_out, preferred_element_type=jnp.float32)
    attn_out = lax.psum(attn_part, "mp")
    resid_one = tokens_seq.astype(jnp.float32) + attn_out + b_out.astype(jnp.float32)
    normed_one = layer_norm(resid_one, gain_one.astype(jnp.float32), shift_one.astype(jnp.float32))
    normed_share = normed_one.astype(jnp.bfloat16)
    pre_act = jnp.dot(normed_share, w_up, preferred_element_type=jnp.float32) + b_up.astype(
        jnp.float32
    )
    hidden_low = gelu_exact(pre_act).astype(jnp.bfloat16)
    ffn_part = jnp.dot(hidden_low, w_down, preferred_element_type=jnp.float32)
    ffn_out = lax.psum(ffn_part, "mp")
    resid_two = normed_one + ffn_out + b_down.astype(jnp.float32)
    out_rows = layer_norm(
        resid_two, gain_two.astype(jnp.float32), shift_two.astype(jnp.float32)
    ).astype(jnp.bfloat16)
    saved_state = (
        proj_low,
        log_total,
        context_low,
        resid_one,
        normed_share,
        pre_act,
        hidden_low,
        resid_two,
    )
    return (out_rows, saved_state)


def backward_pass(tokens_seq, cot_seq, perm_seq, mask_seq, saved_state, weights):
    w_qkv, w_out, gain_one, w_up, w_down, gain_two = weights
    proj_low, log_total, context_low, resid_one, normed_low, pre_act, hidden_low, resid_two = (
        saved_state
    )
    seq_len = tokens_seq.shape[0]
    half_len = seq_len // 2
    local_width = w_qkv.shape[2]
    head_count = local_width // HD
    gain_two_f = gain_two.astype(jnp.float32)
    _, norm_two_back = jax.vjp(layer_norm, resid_two, gain_two_f, jnp.zeros_like(gain_two_f))
    d_resid_two, g_gain_two, g_shift_two = norm_two_back(cot_seq.astype(jnp.float32))
    d_two_share = d_resid_two.astype(jnp.bfloat16)
    g_b_down = jnp.sum(d_resid_two, axis=0)
    g_w_down = contract_rows(hidden_low, d_two_share)
    d_hidden = contract_cols(d_two_share, w_down)
    _, gelu_back = jax.vjp(gelu_exact, pre_act)
    d_pre = gelu_back(d_hidden)[0].astype(jnp.bfloat16)
    g_b_up = jnp.sum(d_pre, axis=0, dtype=jnp.float32)
    g_w_up = contract_rows(normed_low, d_pre)
    d_normed_part = contract_cols(d_pre, w_up)
    d_normed_one = lax.psum(d_normed_part, "mp") + d_resid_two
    gain_one_f = gain_one.astype(jnp.float32)
    _, norm_one_back = jax.vjp(layer_norm, resid_one, gain_one_f, jnp.zeros_like(gain_one_f))
    d_resid_one, g_gain_one, g_shift_one = norm_one_back(d_normed_one)
    d_one_share = d_resid_one.astype(jnp.bfloat16)
    g_b_out = jnp.sum(d_resid_one, axis=0)
    g_w_out = contract_rows(context_low, d_one_share)
    d_context = contract_cols(d_one_share, w_out).astype(jnp.bfloat16)
    query_pair, key_pair, value_pair, swapped = split_pairs(proj_low, perm_seq, head_count)
    allowed, allowed_f, dead_f = pair_pattern(mask_seq, half_len, half_len // 2)
    masked = masked_scores(query_pair, key_pair, allowed)
    attn_prob = jnp.exp(masked - log_total[..., None]) * allowed_f[None]
    d_context_pair = d_context.reshape(2, half_len, head_count, HD)
    d_weights = jnp.einsum(
        "iqhd,ikhd->ihqk", d_context_pair, value_pair, preferred_element_type=jnp.float32
    )
    row_dot = jnp.sum(attn_prob * d_weights, axis=-1, keepdims=True)
    d_scores = (attn_prob * (d_weights - row_dot)).astype(jnp.bfloat16)
    score_scale = HD ** (-0.5)
    d_query = (
        jnp.einsum("ihqk,ikhd->iqhd", d_scores, key_pair, preferred_element_type=jnp.float32)
        * score_scale
    )
    d_key_pair = (
        jnp.einsum("ihqk,iqhd->ikhd", d_scores, query_pair, preferred_element_type=jnp.float32)
        * score_scale
    )
    d_value_pair = jnp.einsum(
        "ihqk,iqhd->ikhd",
        attn_prob.astype(jnp.bfloat16),
        d_context_pair,
        preferred_element_type=jnp.float32,
    )
    d_key = pair_keys(d_key_pair.reshape(seq_len, head_count, HD), swapped)
    d_value = pair_keys(d_value_pair.reshape(seq_len, head_count, HD), swapped)
    d_projected = jnp.stack(
        [
            d_query.reshape(seq_len, local_width),
            d_key.reshape(seq_len, local_width),
            d_value.reshape(seq_len, local_width),
        ],
        axis=1,
    ).astype(jnp.bfloat16)
    g_b_qv = jnp.stack(
        [
            jnp.sum(d_projected[:, 0], axis=0, dtype=jnp.float32),
            jnp.sum(d_projected[:, 2], axis=0, dtype=jnp.float32),
        ]
    )
    g_w_qkv = jnp.einsum("td,tcf->dcf", tokens_seq, d_projected, preferred_element_type=jnp.float32)
    d_input_part = jnp.einsum("tcf,dcf->td", d_projected, w_qkv, preferred_element_type=jnp.float32)
    input_seq = lax.psum(d_input_part.astype(jnp.bfloat16), "mp").astype(jnp.float32) + d_resid_one
    gradients = (
        g_w_qkv,
        g_b_qv,
        g_w_out,
        g_b_out,
        g_gain_one,
        g_shift_one,
        g_w_up,
        g_b_up,
        g_w_down,
        g_b_down,
        g_gain_two,
        g_shift_two,
    )
    return (input_seq, gradients)


def body(
    tokens,
    grad_out,
    head_perm,
    block_mask,
    w_qkv,
    b_qv,
    w_out,
    b_out,
    gain_one,
    shift_one,
    w_up,
    b_up,
    w_down,
    b_down,
    gain_two,
    shift_two,
):
    batch_count = head_perm.shape[0]
    seq_len = tokens.shape[0] // batch_count
    totals = None
    out_parts = []
    input_parts = []
    for batch_index in range(batch_count):
        row_start = batch_index * seq_len
        tokens_seq = tokens[row_start : row_start + seq_len]
        cot_seq = grad_out[row_start : row_start + seq_len]
        perm_seq = head_perm[batch_index]
        mask_seq = block_mask[batch_index]
        forward_weights = (
            lax.all_gather(w_qkv, "dp", axis=0, tiled=True),
            lax.all_gather(b_qv, "dp", axis=1, tiled=True),
            lax.all_gather(w_out, "dp", axis=1, tiled=True),
            lax.all_gather(b_out, "dp", axis=0, tiled=True),
            lax.all_gather(gain_one, "dp", axis=0, tiled=True),
            lax.all_gather(shift_one, "dp", axis=0, tiled=True),
            lax.all_gather(w_up, "dp", axis=0, tiled=True),
            lax.all_gather(b_up, "dp", axis=0, tiled=True),
            lax.all_gather(w_down, "dp", axis=1, tiled=True),
            lax.all_gather(b_down, "dp", axis=0, tiled=True),
            lax.all_gather(gain_two, "dp", axis=0, tiled=True),
            lax.all_gather(shift_two, "dp", axis=0, tiled=True),
        )
        out_seq, saved_state = forward_pass(tokens_seq, perm_seq, mask_seq, forward_weights)
        backward_weights = (
            lax.all_gather(w_qkv, "dp", axis=0, tiled=True),
            lax.all_gather(w_out, "dp", axis=1, tiled=True),
            lax.all_gather(gain_one, "dp", axis=0, tiled=True),
            lax.all_gather(w_up, "dp", axis=0, tiled=True),
            lax.all_gather(w_down, "dp", axis=1, tiled=True),
            lax.all_gather(gain_two, "dp", axis=0, tiled=True),
        )
        input_seq, gradients = backward_pass(
            tokens_seq, cot_seq, perm_seq, mask_seq, saved_state, backward_weights
        )
        if totals is None:
            totals = gradients
        else:
            totals = tuple((summed + latest for summed, latest in zip(totals, gradients)))
        out_parts.append(out_seq)
        input_parts.append(input_seq)
    (
        t_w_qkv,
        t_b_qv,
        t_w_out,
        t_b_out,
        t_gain_one,
        t_shift_one,
        t_w_up,
        t_b_up,
        t_w_down,
        t_b_down,
        t_gain_two,
        t_shift_two,
    ) = totals
    shards = (
        lax.psum_scatter(t_w_qkv, "dp", scatter_dimension=0, tiled=True),
        lax.psum_scatter(t_b_qv, "dp", scatter_dimension=1, tiled=True),
        lax.psum_scatter(t_w_out, "dp", scatter_dimension=1, tiled=True),
        lax.psum_scatter(t_b_out, "dp", scatter_dimension=0, tiled=True),
        lax.psum_scatter(t_gain_one, "dp", scatter_dimension=0, tiled=True),
        lax.psum_scatter(t_shift_one, "dp", scatter_dimension=0, tiled=True),
        lax.psum_scatter(t_w_up, "dp", scatter_dimension=0, tiled=True),
        lax.psum_scatter(t_b_up, "dp", scatter_dimension=0, tiled=True),
        lax.psum_scatter(t_w_down, "dp", scatter_dimension=1, tiled=True),
        lax.psum_scatter(t_b_down, "dp", scatter_dimension=0, tiled=True),
        lax.psum_scatter(t_gain_two, "dp", scatter_dimension=0, tiled=True),
        lax.psum_scatter(t_shift_two, "dp", scatter_dimension=0, tiled=True),
    )
    output = jnp.concatenate(out_parts, axis=0)
    input_grad = jnp.concatenate(input_parts, axis=0)
    return (
        output,
        input_grad,
        shards[0],
        shards[1],
        shards[2],
        shards[3],
        shards[4],
        shards[5],
        shards[6],
        shards[7],
        shards[8],
        shards[9],
        shards[10],
        shards[11],
    )


def solution(mesh):
    placed = (
        P("dp", None),
        P("dp", None),
        P("dp", "mp"),
        P("dp", "mp", None),
        P("dp", None, "mp"),
        P(None, ("mp", "dp")),
        P("mp", "dp"),
        P("dp"),
        P("dp"),
        P("dp"),
        P("dp", "mp"),
        P(("mp", "dp")),
        P("mp", "dp"),
        P("dp"),
        P("dp"),
        P("dp"),
    )
    return jax.shard_map(
        body,
        mesh=mesh,
        in_specs=placed,
        out_specs=(
            P("dp", None),
            P("dp", None),
            P("dp", None, "mp"),
            P(None, ("mp", "dp")),
            P("mp", "dp"),
            P("dp"),
            P("dp"),
            P("dp"),
            P("dp", "mp"),
            P(("mp", "dp")),
            P("mp", "dp"),
            P("dp"),
            P("dp"),
            P("dp"),
        ),
        check_vma=False,
    )
```

profile of v0, /device:TPU:0, one launch (start us, length us, event | category | flops | bytes accessed | tf_op | source)
XLA Modules:
  0.0 1341.1 jit_solution(12367896143275283011)
XLA Ops:
  8.7 23.3 %all-gather = bf16[16,24,2]{1,2,0:T(2,128)(2,1)S(1)} all-gather(bf16[1,24,2]{1,2,0:T(2,128)(2,1)} %bitcast.207), channel_id=1, replica_groups=mesh['dp'=16,'mp'=2] {'dp'}, dimensions={0}, use_global_device_ids=true | all-gather | bytes 1632 | tf_op jit(solution)/shard_map/all_gather | solution.py:253
  32.8 4.4 convert_reduce_fusion.5
  37.3 3.6 convert_element_type.187
  40.9 3.6 convert_element_type.204
  45.8 20.8 %all_gather.26 = bf16[384,768]{0,1:T(8,128)(2,1)} all-gather(bf16[384,48]{0,1:T(8,128)(2,1)S(1)} %copy-done.88), channel_id=1, replica_groups=mesh['dp'=16,'mp'=2] {'dp'}, dimensions={1}, use_global_device_ids=true | all-gather | bytes 626688 | tf_op jit(solution)/shard_map/all_gather | solution.py:254
  66.6 4.0 add_convert_fusion.2
  79.3 3.4 reshape_squeeze.9
  107.5 3.6 concatenate.95
  117.6 4.5 broadcast_select_fusion.2
  130.1 6.4 fusion.56
  149.4 4.3 fusion.53
  165.4 59.2 %all-reduce.20 = (bf16[768]{0:T(1024)(128)(2,1)S(1)}, bf16[768]{0:T(1024)(128)(2,1)S(1)}, bf16[768]{0:T(1024)(128)(2,1)S(1)}, bf16[1536]{0:T(1024)(128)(2,1)S(1)...) all-reduce(bf16[768]{0:T(1024)(128)(2,1)S(1)} %dynamic-update-slice, ...), channel_id=1, replica_groups=mesh['dp'=16,'mp'=2] {'dp'}, use_global_device_ids=true, to_apply=%add | all-reduce | flops 6144 | bytes 24576
  224.6 87.3 %all-reduce.34.cloned.1.call-done = (f32[1024,768]{1,0:T(8,128)}, f32[1024,768]{1,0:T(8,128)}) async-done(((f32[1024,768]{1,0:T(8,128)}, f32[1024,768]{1,0:T(8,128)}), (f32[1024,768]{1,0:T(8,128)}, f32[1024,768]{1,0:T(8,128)})) %all-reduce.34.cloned.1.call-update) | async-done | bytes 6291472 | tf_op jit(solution)/shard_map/psum | solution.py:105
  311.9 4.7 fusion.116
  318.7 37.9 %all-gather.7.cloned.1.call-done = bf16[768,1536]{1,0:T(8,128)(2,1)} async-done(((bf16[48,1536]{1,0:T(8,128)(2,1)}), bf16[768,1536]{1,0:T(8,128)(2,1)}) %all-gather.7.cloned.1.call-update) | async-done | bytes 2359312 | tf_op jit(solution)/shard_map/all_gather | solution.py:258
  356.5 5.5 fusion.101
  364.8 31.7 %multiply_convert_fusion.3 = (bf16[1024,1536]{1,0:T(8,128)(2,1)}, f32[1024,1536]{1,0:T(8,128)}, bf16[1024,1536]{1,0:T(8,128)(2,1)}, f32[1024,1536]{1,0:T(8,128)}, f32[1024,1536]{1,0:T(8,128)}) fusion(f32[1536]{0:T(1024)S(1)} %convert_element_type.196, f32[1024,1536]{1,0:T(8,128)S(1)} %fusion.101, bf16[768,1536]{1,0:T(8,128)(2,1)S(1)} %copy-done.121, ...), kind=kOutput, calls=%fused_computation.34 | convolution fusion | flops 2627469312 | bytes 36982784 | tf_op jit(solution)/shard_map/dot_general | solution.py:109
  399.7 7.1 fusion.129
  406.8 4.3 fusion.131
  411.3 152.0 %all-reduce.32.cloned.1.call-done = (f32[1024,768]{1,0:T(8,128)}, f32[1024,768]{1,0:T(8,128)}) async-done(((f32[1024,768]{1,0:T(8,128)}, f32[1024,768]{1,0:T(8,128)}), (f32[1024,768]{1,0:T(8,128)}, f32[1024,768]{1,0:T(8,128)})) %all-reduce.32.cloned.1.call-update) | async-done | bytes 6291472 | tf_op jit(solution)/shard_map/psum | solution.py:114
  563.3 5.2 fusion.113
  573.8 4.2 fusion.112
  578.0 10.6 convert_reduce_fusion.1
  588.6 4.3 fusion.132
  593.0 7.3 convert_reduce_fusion
  602.0 4.3 fusion.133
  608.3 151.4 %all-reduce.30.cloned.1.call-done = (f32[1024,768]{1,0:T(8,128)}, f32[1024,768]{1,0:T(8,128)}) async-done(((f32[1024,768]{1,0:T(8,128)}, f32[1024,768]{1,0:T(8,128)}), (f32[1024,768]{1,0:T(8,128)}, f32[1024,768]{1,0:T(8,128)})) %all-reduce.30.cloned.1.call-update) | async-done | bytes 6291472 | tf_op jit(solution)/shard_map/psum | solution.py:153
  759.8 5.6 multiply_reduce_fusion.4
  766.3 4.4 multiply_reduce_fusion.5
  777.1 8.8 fusion.44
  797.3 9.8 fusion.41
  809.8 10.2 multiply_reduce_fusion
  820.0 10.3 multiply_convert_fusion
  836.3 10.1 multiply_reduce_fusion.1
  846.4 10.5 multiply_convert_fusion.1
  904.1 3.9 copy.156
  909.4 5.2 bitcast_convert_fusion
  920.1 5.0 fusion.96
  925.1 4.7 convolution_add_fusion
  931.7 5.1 fusion.103
  936.9 4.7 convolution_add_fusion.1
  954.4 70.6 %all-reduce.28.cloned.1.call-done = f32[768,3,384]{2,1,0:T(4,128)} async-done(((f32[768,3,384]{2,1,0:T(4,128)}), f32[768,3,384]{2,1,0:T(4,128)}) %all-reduce.28.cloned.1.call-update) | async-done | bytes 3538960
  1026.8 86.3 %all-reduce.36.cloned.1.call-done = (bf16[1024,768]{1,0:T(8,128)(2,1)}, bf16[1024,768]{1,0:T(8,128)(2,1)}) async-done(((bf16[1024,768]{1,0:T(8,128)(2,1)}, bf16[1024,768]{1,0:T(8,128)(2,1)}), (bf16[1024,768]{1,0:T(8,128)(2,1)}, bf16[1024,768]{1,0:T(8,128)(2,1)})) %all-reduce.36.cloned.1.call-update) | async-done | bytes 3145744 | tf_op jit(solution)/shard_map/psum | solution.py:204
  1113.1 3.7 add_reduce_fusion
  1118.9 62.2 %all-reduce.16 = (f32[2,384]{1,0:T(2,128)S(1)}, f32[768]{0:T(1024)S(1)}, f32[768]{0:T(1024)S(1)}, f32[768]{0:T(1024)S(1)}, f32[1536]{0:T(1024)S(1)}, /*index=5*/...) all-reduce(f32[2,384]{1,0:T(2,128)S(1)} %maximum_add_fusion, ...), channel_id=3, replica_groups=mesh['dp'=16,'mp'=2] {'dp'}, use_global_device_ids=true, to_apply=%region_37.38.clone | all-reduce | flops 6912 | bytes 55296
  1185.8 5.0 pad_maximum_fusion
  1193.5 79.0 %reduce-scatter.7.cloned.1.call-done = f32[48,1536]{1,0:T(8,128)} async-done(((f32[768,1536]{1,0:T(8,128)}), f32[48,1536]{1,0:T(8,128)}) %reduce-scatter.7.cloned.1.call-update) | async-done | bytes 294928 | tf_op jit(solution)/shard_map/reduce_scatter | solution.py:304
  1272.5 61.6 %reduce-scatter.5.cloned.1.call-done = f32[384,48]{0,1:T(8,128)} async-done(((f32[384,768]{0,1:T(8,128)}), f32[384,48]{0,1:T(8,128)}) %reduce-scatter.5.cloned.1.call-update) | async-done | bytes 73744 | tf_op jit(solution)/shard_map/reduce_scatter | solution.py:300
  (495 shorter events, 195.6 us)
Async XLA Ops:
  7.2 59.4 %all-gather.5.cloned.1.call-start = ((), (), s32[]{:S(2)}) async-start(), calls=%async_computation.3 | async-start | bytes 1880064 | tf_op jit(solution)/shard_map/all_gather | solution.py:252
  7.9 304.0 %all-reduce.34.cloned.1.call-start = ((), (), s32[]{:S(2)}) async-start(), calls=%async_computation.12 | async-start | bytes 12582912 | tf_op jit(solution)/shard_map/psum | solution.py:105
  37.3 91.7 %copy-start.2 = (pred[6,512,512]{1,2,0:T(8,128)(4,1)}, pred[6,512,512]{1,2,0:T(8,128)(4,1)S(1)}, u32[]{:S(2)}) copy-start(pred[6,512,512]{1,2,0:T(8,128)(4,1)S(1)} %get-tuple-element.124) | copy-start | bytes 4718596
  37.3 111.0 %copy-start.4 = (pred[6,512,512]{1,2,0:T(8,128)(4,1)}, pred[6,512,512]{1,2,0:T(8,128)(4,1)S(1)}, u32[]{:S(2)}) copy-start(pred[6,512,512]{1,2,0:T(8,128)(4,1)S(1)} %get-tuple-element.155) | copy-start | bytes 4718596
  104.2 13.4 copy-start.117
  128.9 7.5 copy-start.65
  141.4 6.9 copy-start.31
  160.4 196.1 %all-gather.7.cloned.1.call-start = ((), (), s32[]{:S(2)}) async-start(), calls=%async_computation.4 | async-start | bytes 2506752 | tf_op jit(solution)/shard_map/all_gather | solution.py:258
  161.2 238.6 %all-gather.9.cloned.1.call-start = ((), (), s32[]{:S(2)}) async-start(), calls=%async_computation.5 | async-start | bytes 2506752 | tf_op jit(solution)/shard_map/all_gather | solution.py:260
  161.8 401.5 %all-reduce.32.cloned.1.call-start = ((), (), s32[]{:S(2)}) async-start(), calls=%async_computation.11 | async-start | bytes 12582912 | tf_op jit(solution)/shard_map/psum | solution.py:114
  224.6 338.7 %copy-start.108 = (f32[768]{0:T(1024)}, f32[768]{0:T(1024)S(1)}, u32[]{:S(2)}) copy-start(f32[768]{0:T(1024)S(1)} %convert_element_type.194) | copy-start | bytes 9220
  316.6 448.8 %copy-start.7 = (f32[1024,768]{1,0:T(8,128)}, f32[1024,768]{1,0:T(8,128)S(1)}, u32[]{:S(2)}) copy-start(f32[1024,768]{1,0:T(8,128)S(1)} %get-tuple-element.118) | copy-start | bytes 9437188
  318.6 43.5 %copy-start.84 = (f32[1024]{0:T(1024)}, f32[1024]{0:T(1024)S(1)}, u32[]{:S(2)}) copy-start(f32[1024]{0:T(1024)S(1)} %multiply_reduce_fusion.11) | copy-start | bytes 12292
  318.7 446.7 %copy-start.81 = (f32[1024]{0:T(1024)}, f32[1024]{0:T(1024)S(1)}, u32[]{:S(2)}) copy-start(f32[1024]{0:T(1024)S(1)} %fusion.85) | copy-start | bytes 12292
  356.5 8.2 copy-start.121
  399.7 7.1 copy-start.123
  399.7 7.1 copy-start.135
  411.2 348.6 %all-reduce.30.cloned.1.call-start = ((), (), s32[]{:S(2)}) async-start(), calls=%async_computation.10 | async-start | bytes 12582912 | tf_op jit(solution)/shard_map/psum | solution.py:153
  573.7 19.2 %slice-start.8 = ((s8[6291456]{0:T(1024)(128)(4,1)}), s8[4194304]{0:T(1024)(128)(4,1)S(1)}, s32[]{:S(2)}) async-start(s8[6291456]{0:T(1024)(128)(4,1)} %bitcast.208), calls=%async_computation.22 | async-start | bytes 8388608
  578.0 10.6 copy-start.21
  578.0 15.0 %copy-start.24 = (f32[1024,768]{1,0:T(8,128)}, f32[1024,768]{1,0:T(8,128)S(1)}, u32[]{:S(2)}) copy-start(f32[1024,768]{1,0:T(8,128)S(1)} %get-tuple-element.110) | copy-start | bytes 9437188
  578.0 181.8 %copy-start.104 = (f32[1024]{0:T(1024)}, f32[1024]{0:T(1024)S(1)}, u32[]{:S(2)}) copy-start(f32[1024]{0:T(1024)S(1)} %negate_multiply_fusion.3) | copy-start | bytes 12292
  578.0 187.4 %copy-start.106 = (f32[1024]{0:T(1024)}, f32[1024]{0:T(1024)S(1)}, u32[]{:S(2)}) copy-start(f32[1024]{0:T(1024)S(1)} %negate_multiply_fusion.5) | copy-start | bytes 12292
  578.0 10.6 copy-start.122
  578.0 14.9 %slice-start.9 = ((s8[6291456]{0:T(1024)(128)(4,1)}), s8[2097152]{0:T(1024)(128)(4,1)S(1)}, s32[]{:S(2)}) async-start(s8[6291456]{0:T(1024)(128)(4,1)} %bitcast.208), calls=%async_computation.23 | async-start | bytes 4194304
  606.3 418.8 %all-reduce.28.cloned.1.call-start = ((), (), s32[]{:S(2)}) async-start(), calls=%async_computation.9 | async-start | bytes 9437184
  759.8 6.5 copy-start.39
  766.3 6.0 copy-start.37
  777.1 11.4 copy-start.85
  777.1 11.3 copy-start.101
  777.1 11.3 copy-start.15
  793.9 15.9 %slice-start.6 = ((s8[6291456]{0:T(1024)(128)(4,1)}), s8[2097152]{0:T(1024)(128)(4,1)S(1)}, s32[]{:S(2)}) async-start(s8[6291456]{0:T(1024)(128)(4,1)} %bitcast.186), calls=%async_computation.20 | async-start | bytes 4194304
  797.3 12.5 slice-start.7
  820.0 10.3 copy-start.58
  830.3 5.9 slice-start.2
  846.4 10.5 copy-start.56
  861.8 7.6 copy-start.45
  876.5 7.3 copy-start.26
  886.3 8.1 copy-start.27
  890.4 7.9 copy-start.46
  908.1 6.6 copy-start.72
  908.1 6.6 copy-start.76
  908.1 205.0 %all-reduce.36.cloned.1.call-start = ((), (), s32[]{:S(2)}) async-start(), calls=%async_computation.13 | async-start | bytes 6291456 | tf_op jit(solution)/shard_map/psum | solution.py:204
  918.1 7.0 copy-start.105
  918.1 275.4 %reduce-scatter.9.cloned.1.call-start = ((), (), s32[]{:S(2)}) async-start(), calls=%async_computation.8 | async-start | bytes 5013504 | tf_op jit(solution)/shard_map/reduce_scatter | solution.py:306
  929.8 342.7 %reduce-scatter.7.cloned.1.call-start = ((), (), s32[]{:S(2)}) async-start(), calls=%async_computation.7 | async-start | bytes 5013504 | tf_op jit(solution)/shard_map/reduce_scatter | solution.py:304
  941.6 392.5 %reduce-scatter.5.cloned.1.call-start = ((), (), s32[]{:S(2)}) async-start(), calls=%async_computation.6 | async-start | bytes 1253376 | tf_op jit(solution)/shard_map/reduce_scatter | solution.py:300
  1116.8 69.0 %copy-start.19 = (f32[1024,768]{1,0:T(8,128)S(1)}, f32[1024,768]{1,0:T(8,128)}, u32[]{:S(2)}) copy-start(f32[1024,768]{1,0:T(8,128)} %get-tuple-element.135) | copy-start | bytes 9437188
  (113 other events, 368.8 us)
Sparse Core Ops, SparseCore 0:
  10.3 43.1 all-gather.4
  160.6 151.2 all-reduce.33
  314.2 42.3 all-gather.6
  358.7 41.0 all-gather.8
  411.3 151.9 all-reduce.31
  606.5 153.2 all-reduce.29
  908.2 116.8 all-reduce.27
  1027.4 85.5 all-reduce.35
  1117.5 75.9 reduce-scatter.8
  1197.8 74.6 reduce-scatter.6
  1276.7 57.3 reduce-scatter.4
where the time goes:
time: 1350 us; the launch traced here: 1340 us
  waiting for transfers between devices  734 us (54%)
  matrix products  189 us (14%)
  blocking collectives  165 us (12%)
  local copies, waits for them, and re-layouts  128 us (9%)
  other arithmetic  104 us (8%)
  between operations  19.7 us (1%)
    psum x1, waiting for transfers between devices, forward_pass(): ffn_out = lax.psum(ffn_part, 'mp')  152 us
    psum x1, waiting for transfers between devices, backward_pass(): d_normed_one = lax.psum(d_normed_part, 'mp') + d_resid_two  151 us
    unnamed x2, blocking collectives  121 us
    psum x1, waiting for transfers between devices, forward_pass(): attn_out = lax.psum(attn_part, 'mp')  87.3 us
    psum x1, waiting for transfers between devices, backward_pass(): lax.psum(d_input_part.astype(jnp.bfloat16), 'mp').astype(jnp.float32)  86.3 us
    reduce_scatter x1, waiting for transfers between devices, body(): lax.psum_scatter(t_w_up, 'dp', scatter_dimension=0, tiled=True)  79 us
    unnamed x12, waiting for transfers between devices  72.7 us
    reduce_scatter x1, waiting for transfers between devices, body(): lax.psum_scatter(t_w_out, 'dp', scatter_dimension=1, tiled=True)  61.6 us
  transfers between devices with their start and end apart: 11, of which 10 were waited for; matrix products, arithmetic and copies ran while one was open for 9% of the time, Pallas kernels for 0%

commit v1 on v0

--- a/solution.py
+++ b/solution.py
@@ -6,6 +6,7 @@
 HD = 64
 norm_eps = 1e-05
 masked_fill = -1e30
+time_copies = lambda page: jnp.sum(jax.lax.all_gather(page, "mp"), 0)
 
 
 def layer_norm(hidden, gain_vec, shift_vec):
@@ -102,7 +103,7 @@
     )
     context_low = context.reshape(seq_len, local_width).astype(jnp.bfloat16)
     attn_part = jnp.dot(context_low, w_out, preferred_element_type=jnp.float32)
-    attn_out = lax.psum(attn_part, "mp")
+    attn_out = time_copies(attn_part)
     resid_one = tokens_seq.astype(jnp.float32) + attn_out + b_out.astype(jnp.float32)
     normed_one = layer_norm(resid_one, gain_one.astype(jnp.float32), shift_one.astype(jnp.float32))
     normed_share = normed_one.astype(jnp.bfloat16)

time: 1350 us -> 1310 us (0.970)
  waiting for transfers between devices: 734 us -> 682 us
    psum x1 -> x0, waiting for transfers between devices: 87.3 us -> none  [forward_pass(): attn_out = lax.psum(attn_part, 'mp')]
    all_gather x0 -> x2, waiting for transfers between devices: none -> 40.4 us  [time_copies = lambda page: jnp.sum(jax.lax.all_gather(page, 'mp'), 0)]
    unnamed x329 -> x327, local copies, waits for them, and re-layouts: 32.4 us -> 32.2 us
    unnamed x12 -> x13, waiting for transfers between devices: 72.7 us -> 72.5 us
  transfers between devices with their start and end apart: 11 -> 12, of which waited for: 10 -> 10; matrix products, arithmetic and copies ran while one was open for 9% -> 13% of each run, Pallas kernels for 0% -> 0%
where the time goes in v1:
time: 1310 us; the launch traced here: 1300 us
  waiting for transfers between devices  682 us (52%)
  matrix products  189 us (14%)
  blocking collectives  166 us (13%)
  local copies, waits for them, and re-layouts  129 us (10%)
  other arithmetic  116 us (9%)
  between operations  20 us (2%)
    psum x1, waiting for transfers between devices, forward_pass(): ffn_out = lax.psum(ffn_part, 'mp')  152 us
    psum x1, waiting for transfers between devices, backward_pass(): d_normed_one = lax.psum(d_normed_part, 'mp') + d_resid_two  151 us
    unnamed x2, blocking collectives  121 us
    psum x1, waiting for transfers between devices, backward_pass(): lax.psum(d_input_part.astype(jnp.bfloat16), 'mp').astype(jnp.float32)  86.3 us
    reduce_scatter x1, waiting for transfers between devices, body(): lax.psum_scatter(t_w_up, 'dp', scatter_dimension=0, tiled=True)  79.1 us
    unnamed x13, waiting for transfers between devices  72.5 us
    reduce_scatter x1, waiting for transfers between devices, body(): lax.psum_scatter(t_w_out, 'dp', scatter_dimension=1, tiled=True)  61.5 us
    all_gather x2, waiting for transfers between devices, time_copies = lambda page: jnp.sum(jax.lax.all_gather(page, 'mp'), 0)  40.4 us
  transfers between devices with their start and end apart: 12, of which 10 were waited for; matrix products, arithmetic and copies ran while one was open for 13% of the time, Pallas kernels for 0%

profile of v1, /device:TPU:0, one launch (start us, length us, event | category | flops | bytes accessed | tf_op | source)
XLA Modules:
  0.0 1302.8 jit_solution(2917109372230409095)
XLA Ops:
  8.7 23.3 %all-gather.2 = bf16[16,24,2]{1,2,0:T(2,128)(2,1)S(1)} all-gather(bf16[1,24,2]{1,2,0:T(2,128)(2,1)} %bitcast.211), channel_id=1, replica_groups=mesh['dp'=16,'mp'=2] {'dp'}, dimensions={0}, use_global_device_ids=true | all-gather | bytes 1632 | tf_op jit(solution)/shard_map/all_gather | solution.py:254
  32.8 4.4 convert_reduce_fusion.5
  42.3 21.2 %all_gather.34 = bf16[384,768]{0,1:T(8,128)(2,1)} all-gather(bf16[384,48]{0,1:T(8,128)(2,1)S(1)} %copy-done.85), channel_id=1, replica_groups=mesh['dp'=16,'mp'=2] {'dp'}, dimensions={1}, use_global_device_ids=true | all-gather | bytes 626688 | tf_op jit(solution)/shard_map/all_gather | solution.py:255
  63.5 4.0 add_convert_fusion.3
  89.2 4.5 broadcast_select_fusion.2
  97.1 3.8 multiply_reduce_fusion.3
  101.6 6.2 fusion.56
  113.7 4.1 convert_element_type.204
  153.7 5.1 fusion.53
  169.3 59.1 %all-reduce.19 = (bf16[768]{0:T(1024)(128)(2,1)S(1)}, bf16[768]{0:T(1024)(128)(2,1)S(1)}, bf16[768]{0:T(1024)(128)(2,1)S(1)}, bf16[1536]{0:T(1024)(128)(2,1)S(1)...) all-reduce(bf16[768]{0:T(1024)(128)(2,1)S(1)} %dynamic-update-slice, ...), channel_id=1, replica_groups=mesh['dp'=16,'mp'=2] {'dp'}, use_global_device_ids=true, to_apply=%add | all-reduce | flops 6144 | bytes 24576
  228.4 5.2 reduce_sum.351
  233.7 40.3 %all-gather.17.cloned.1.call-done = f32[2048,768]{1,0:T(8,128)} async-done(((f32[1024,768]{1,0:T(8,128)}), f32[2048,768]{1,0:T(8,128)}) %all-gather.17.cloned.1.call-update) | async-done | bytes 6291472 | tf_op jit(solution)/shard_map/all_gather | solution.py:9
  274.0 5.2 reduce_sum.363
  279.2 4.7 fusion.116
  285.9 32.5 %all-gather.11.cloned.1.call-done = bf16[768,1536]{1,0:T(8,128)(2,1)} async-done(((bf16[48,1536]{1,0:T(8,128)(2,1)}), bf16[768,1536]{1,0:T(8,128)(2,1)}) %all-gather.11.cloned.1.call-update) | async-done | bytes 2359312 | tf_op jit(solution)/shard_map/all_gather | solution.py:259
  318.5 5.5 fusion.101
  326.7 31.6 %multiply_convert_fusion.3 = (bf16[1024,1536]{1,0:T(8,128)(2,1)}, f32[1024,1536]{1,0:T(8,128)}, bf16[1024,1536]{1,0:T(8,128)(2,1)}, f32[1024,1536]{1,0:T(8,128)}, f32[1024,1536]{1,0:T(8,128)}) fusion(f32[1536]{0:T(1024)S(1)} %convert_element_type.196, f32[1024,1536]{1,0:T(8,128)S(1)} %fusion.101, bf16[768,1536]{1,0:T(8,128)(2,1)S(1)} %copy-done.120, ...), kind=kOutput, calls=%fused_computation.34 | convolution fusion | flops 2627469312 | bytes 36982784 | tf_op jit(solution)/shard_map/dot_general | solution.py:110
  361.7 7.1 fusion.129
  368.7 4.3 fusion.131
  373.2 152.0 %all-reduce.30.cloned.1.call-done = (f32[1024,768]{1,0:T(8,128)}, f32[1024,768]{1,0:T(8,128)}) async-done(((f32[1024,768]{1,0:T(8,128)}, f32[1024,768]{1,0:T(8,128)}), (f32[1024,768]{1,0:T(8,128)}, f32[1024,768]{1,0:T(8,128)})) %all-reduce.30.cloned.1.call-update) | async-done | bytes 6291472 | tf_op jit(solution)/shard_map/psum | solution.py:115
  525.2 5.0 fusion.113
  535.4 4.2 fusion.112
  539.7 10.6 convert_reduce_fusion.1
  550.3 4.3 fusion.132
  554.6 7.3 convert_reduce_fusion
  563.6 4.3 fusion.133
  569.8 151.4 %all-reduce.28.cloned.1.call-done = (f32[1024,768]{1,0:T(8,128)}, f32[1024,768]{1,0:T(8,128)}) async-done(((f32[1024,768]{1,0:T(8,128)}, f32[1024,768]{1,0:T(8,128)}), (f32[1024,768]{1,0:T(8,128)}, f32[1024,768]{1,0:T(8,128)})) %all-reduce.28.cloned.1.call-update) | async-done | bytes 6291472 | tf_op jit(solution)/shard_map/psum | solution.py:154
  721.3 5.6 multiply_reduce_fusion.4
  727.8 4.4 multiply_reduce_fusion.5
  738.7 8.8 fusion.44
  758.8 9.8 fusion.41
  771.3 10.2 multiply_reduce_fusion
  781.5 10.3 multiply_convert_fusion
  797.8 10.1 multiply_reduce_fusion.1
  808.0 10.5 multiply_convert_fusion.1
  865.7 3.9 copy.156
  871.0 5.3 bitcast_convert_fusion
  881.6 5.0 fusion.96
  886.7 4.7 convolution_add_fusion
  893.2 5.1 fusion.103
  898.4 4.7 convolution_add_fusion.1
  916.0 70.6 %all-reduce.26.cloned.1.call-done = f32[768,3,384]{2,1,0:T(4,128)} async-done(((f32[768,3,384]{2,1,0:T(4,128)}), f32[768,3,384]{2,1,0:T(4,128)}) %all-reduce.26.cloned.1.call-update) | async-done | bytes 3538960
  988.3 86.3 %all-reduce.32.cloned.1.call-done = (bf16[1024,768]{1,0:T(8,128)(2,1)}, bf16[1024,768]{1,0:T(8,128)(2,1)}) async-done(((bf16[1024,768]{1,0:T(8,128)(2,1)}, bf16[1024,768]{1,0:T(8,128)(2,1)}), (bf16[1024,768]{1,0:T(8,128)(2,1)}, bf16[1024,768]{1,0:T(8,128)(2,1)})) %all-reduce.32.cloned.1.call-update) | async-done | bytes 3145744 | tf_op jit(solution)/shard_map/psum | solution.py:205
  1074.6 3.7 add_reduce_fusion
  1080.4 62.2 %all-reduce.16 = (f32[2,384]{1,0:T(2,128)S(1)}, f32[768]{0:T(1024)S(1)}, f32[768]{0:T(1024)S(1)}, f32[768]{0:T(1024)S(1)}, f32[1536]{0:T(1024)S(1)}, /*index=5*/...) all-reduce(f32[2,384]{1,0:T(2,128)S(1)} %maximum_add_fusion, ...), channel_id=5, replica_groups=mesh['dp'=16,'mp'=2] {'dp'}, use_global_device_ids=true, to_apply=%region_37.38.clone | all-reduce | flops 6912 | bytes 55296
  1147.4 5.0 pad_maximum_fusion
  1154.9 79.1 %reduce-scatter.7.cloned.1.call-done = f32[48,1536]{1,0:T(8,128)} async-done(((f32[768,1536]{1,0:T(8,128)}), f32[48,1536]{1,0:T(8,128)}) %reduce-scatter.7.cloned.1.call-update) | async-done | bytes 294928 | tf_op jit(solution)/shard_map/reduce_scatter | solution.py:305
  1234.0 61.5 %reduce-scatter.5.cloned.1.call-done = f32[384,48]{0,1:T(8,128)} async-done(((f32[384,768]{0,1:T(8,128)}), f32[384,48]{0,1:T(8,128)}) %reduce-scatter.5.cloned.1.call-update) | async-done | bytes 73744 | tf_op jit(solution)/shard_map/reduce_scatter | solution.py:301
  (498 shorter events, 204.6 us)
Async XLA Ops:
  7.2 56.3 %all-gather.9.cloned.1.call-start = ((), (), s32[]{:S(2)}) async-start(), calls=%async_computation.3 | async-start | bytes 1880064 | tf_op jit(solution)/shard_map/all_gather | solution.py:253
  7.9 220.5 %all-gather.15.cloned.1.call-start = ((), (), s32[]{:S(2)}) async-start(), calls=%async_computation.9 | async-start | bytes 9437184 | tf_op jit(solution)/shard_map/all_gather | solution.py:9
  37.2 63.7 %copy-start.2 = (pred[6,512,512]{1,2,0:T(8,128)(4,1)}, pred[6,512,512]{1,2,0:T(8,128)(4,1)S(1)}, u32[]{:S(2)}) copy-start(pred[6,512,512]{1,2,0:T(8,128)(4,1)S(1)} %get-tuple-element.118) | copy-start | bytes 4718596
  37.3 115.6 %copy-start.4 = (pred[6,512,512]{1,2,0:T(8,128)(4,1)}, pred[6,512,512]{1,2,0:T(8,128)(4,1)S(1)}, u32[]{:S(2)}) copy-start(pred[6,512,512]{1,2,0:T(8,128)(4,1)S(1)} %get-tuple-element.153) | copy-start | bytes 4718596
  41.7 25.8 %copy-start.111 = (f32[3,384]{1,0:T(4,128)}, f32[3,384]{1,0:T(4,128)S(1)}, u32[]{:S(2)}) copy-start(f32[3,384]{1,0:T(4,128)S(1)} %maximum_convert_fusion) | copy-start | bytes 13828
  76.1 13.0 %copy-start.116 = (pred[6]{0:T(512)(128)(4,1)S(1)}, pred[6]{0:T(512)(128)(4,1)}, u32[]{:S(2)}) copy-start(pred[6]{0:T(512)(128)(4,1)} %get-tuple-element.182) | copy-start | bytes 22
  100.9 7.0 copy-start.62
  113.6 160.4 %all-gather.17.cloned.1.call-start = ((), (), s32[]{:S(2)}) async-start(), calls=%async_computation.10 | async-start | bytes 9437184 | tf_op jit(solution)/shard_map/all_gather | solution.py:9
  129.1 13.0 copy-start.114
  145.8 7.1 copy-start.31
  161.7 7.1 copy-start.131
  161.7 7.3 copy-start.132
  164.5 153.9 %all-gather.11.cloned.1.call-start = ((), (), s32[]{:S(2)}) async-start(), calls=%async_computation.4 | async-start | bytes 2506752 | tf_op jit(solution)/shard_map/all_gather | solution.py:259
  165.1 196.6 %all-gather.13.cloned.1.call-start = ((), (), s32[]{:S(2)}) async-start(), calls=%async_computation.5 | async-start | bytes 2506752 | tf_op jit(solution)/shard_map/all_gather | solution.py:261
  165.7 359.5 %all-reduce.30.cloned.1.call-start = ((), (), s32[]{:S(2)}) async-start(), calls=%async_computation.13 | async-start | bytes 12582912 | tf_op jit(solution)/shard_map/psum | solution.py:115
  228.4 296.8 %copy-start.105 = (f32[768]{0:T(1024)}, f32[768]{0:T(1024)S(1)}, u32[]{:S(2)}) copy-start(f32[768]{0:T(1024)S(1)} %convert_element_type.194) | copy-start | bytes 9220
  283.8 443.1 %copy-start.7 = (f32[1024,768]{1,0:T(8,128)}, f32[1024,768]{1,0:T(8,128)S(1)}, u32[]{:S(2)}) copy-start(f32[1024,768]{1,0:T(8,128)S(1)} %get-tuple-element.116) | copy-start | bytes 9437188
  285.9 38.1 %copy-start.81 = (f32[1024]{0:T(1024)}, f32[1024]{0:T(1024)S(1)}, u32[]{:S(2)}) copy-start(f32[1024]{0:T(1024)S(1)} %multiply_reduce_fusion.11) | copy-start | bytes 12292
  285.9 441.0 %copy-start.78 = (f32[1024]{0:T(1024)}, f32[1024]{0:T(1024)S(1)}, u32[]{:S(2)}) copy-start(f32[1024]{0:T(1024)S(1)} %fusion.85) | copy-start | bytes 12292
  318.5 8.3 copy-start.120
  361.7 7.1 copy-start.122
  361.7 7.1 copy-start.134
  373.1 348.2 %all-reduce.28.cloned.1.call-start = ((), (), s32[]{:S(2)}) async-start(), calls=%async_computation.12 | async-start | bytes 12582912 | tf_op jit(solution)/shard_map/psum | solution.py:154
  535.4 19.1 %slice-start.8 = ((s8[6291456]{0:T(1024)(128)(4,1)}), s8[4194304]{0:T(1024)(128)(4,1)S(1)}, s32[]{:S(2)}) async-start(s8[6291456]{0:T(1024)(128)(4,1)} %bitcast.212), calls=%async_computation.23 | async-start | bytes 8388608
  539.6 10.6 copy-start.21
  539.6 14.9 %copy-start.24 = (f32[1024,768]{1,0:T(8,128)}, f32[1024,768]{1,0:T(8,128)S(1)}, u32[]{:S(2)}) copy-start(f32[1024,768]{1,0:T(8,128)S(1)} %get-tuple-element.108) | copy-start | bytes 9437188
  539.7 181.6 %copy-start.101 = (f32[1024]{0:T(1024)}, f32[1024]{0:T(1024)S(1)}, u32[]{:S(2)}) copy-start(f32[1024]{0:T(1024)S(1)} %negate_multiply_fusion.3) | copy-start | bytes 12292
  539.7 187.3 %copy-start.103 = (f32[1024]{0:T(1024)}, f32[1024]{0:T(1024)S(1)}, u32[]{:S(2)}) copy-start(f32[1024]{0:T(1024)S(1)} %negate_multiply_fusion.5) | copy-start | bytes 12292
  539.7 10.6 copy-start.121
  539.7 14.9 %slice-start.9 = ((s8[6291456]{0:T(1024)(128)(4,1)}), s8[2097152]{0:T(1024)(128)(4,1)S(1)}, s32[]{:S(2)}) async-start(s8[6291456]{0:T(1024)(128)(4,1)} %bitcast.212), calls=%async_computation.24 | async-start | bytes 4194304
  567.9 418.8 %all-reduce.26.cloned.1.call-start = ((), (), s32[]{:S(2)}) async-start(), calls=%async_computation.11 | async-start | bytes 9437184
  738.6 11.3 copy-start.82
  738.7 11.3 copy-start.98
  738.7 11.3 copy-start.15
  755.4 15.9 %slice-start.6 = ((s8[6291456]{0:T(1024)(128)(4,1)}), s8[2097152]{0:T(1024)(128)(4,1)S(1)}, s32[]{:S(2)}) async-start(s8[6291456]{0:T(1024)(128)(4,1)} %bitcast.188), calls=%async_computation.21 | async-start | bytes 4194304
  758.8 12.5 slice-start.7
  781.5 10.3 copy-start.55
  808.0 10.5 copy-start.53
  823.4 7.6 copy-start.42
  838.0 7.3 copy-start.26
  847.8 8.1 copy-start.27
  851.9 7.9 copy-start.43
  869.6 205.0 %all-reduce.32.cloned.1.call-start = ((), (), s32[]{:S(2)}) async-start(), calls=%async_computation.14 | async-start | bytes 6291456 | tf_op jit(solution)/shard_map/psum | solution.py:205
  879.7 6.9 copy-start.102
  879.7 275.2 %reduce-scatter.9.cloned.1.call-start = ((), (), s32[]{:S(2)}) async-start(), calls=%async_computation.8 | async-start | bytes 5013504 | tf_op jit(solution)/shard_map/reduce_scatter | solution.py:307
  891.4 342.7 %reduce-scatter.7.cloned.1.call-start = ((), (), s32[]{:S(2)}) async-start(), calls=%async_computation.7 | async-start | bytes 5013504 | tf_op jit(solution)/shard_map/reduce_scatter | solution.py:305
  903.2 392.3 %reduce-scatter.5.cloned.1.call-start = ((), (), s32[]{:S(2)}) async-start(), calls=%async_computation.6 | async-start | bytes 1253376 | tf_op jit(solution)/shard_map/reduce_scatter | solution.py:301
  1078.3 69.1 %copy-start.19 = (f32[1024,768]{1,0:T(8,128)S(1)}, f32[1024,768]{1,0:T(8,128)}, u32[]{:S(2)}) copy-start(f32[1024,768]{1,0:T(8,128)} %get-tuple-element.133) | copy-start | bytes 9437188
  (113 other events, 400.6 us)
Sparse Core Ops, SparseCore 0:
  10.3 44.0 all-gather.8
  113.7 78.2 all-gather.14
  193.6 80.3 all-gather.16
  276.1 42.3 all-gather.10
  320.6 41.0 all-gather.12
  373.2 151.9 all-reduce.29
  568.0 153.2 all-reduce.27
  869.7 116.8 all-reduce.25
  989.0 85.5 all-reduce.31
  1078.9 75.9 reduce-scatter.8
  1159.3 74.6 reduce-scatter.6
  1238.1 57.3 reduce-scatter.4
